TPU v7x, 32 devices: a whole 2x2x4 slice. The times are simulated.
32 devices in a mesh: section: 8 (over z, core), tensor: 2 (over x), replica: 2 (over y).
Axes of the slice: x: 2, y: 2, z: 4, core: 2. Of those that a mesh axis runs over, the one named last changes fastest.
Arguments:
- pool_inputs: bfloat16 [8, 256, 2, 1408], P('section', 'replica', None, 'tensor'), may hold values from -6 to 6
- pool_mixed: bfloat16 [8, 256, 1408], P('section', 'replica'), may hold values from -6 to 6
- crop_ids: int32 [8, 8, 128], P('section', 'replica'), may hold values from 0 to 127
- incoming: bfloat16 [8, 256, 1408], P('section', 'replica', 'tensor'), may hold values from -6 to 6
- loss_grads: bfloat16 [3, 256, 1408], P(None, 'replica', 'tensor'), may hold values from -6 to 6
- w_proj: bfloat16 [8, 2, 1408, 1408], P('section', None, ('tensor', 'replica')), may hold values from -0.109375 to 0.109375
- w_up: bfloat16 [8, 1408, 3072], P('section', None, ('tensor', 'replica')), may hold values from -0.15625 to 0.15625
- w_down: bfloat16 [8, 3072, 1408], P('section', ('tensor', 'replica')), may hold values from -0.109375 to 0.109375
Outputs:
- grad_proj: bfloat16 [8, 2, 1408, 1408], P('section', None, ('tensor', 'replica'))
- grad_up: bfloat16 [8, 1408, 3072], P('section', None, ('tensor', 'replica'))
- grad_down: bfloat16 [8, 3072, 1408], P('section', ('tensor', 'replica'))
- outgoing: bfloat16 [8, 256, 2, 1408], P('section', 'replica', None, 'tensor')
All inputs are finite; a program needn't handle non-finite values.
Results may differ from a plain program's by a relative error of at most 0.02.
Values may be sent and summed in bfloat16 or wider, within the bound.
A program may use at most 128 MiB of HBM per device.

v0:
```python
import functools

import jax
import jax.numpy as jnp
from jax import lax
from jax.experimental import pallas as pl
from jax.experimental.pallas import tpu as pltpu
from jax.sharding import PartitionSpec as P

gelu_scale = 0.7978845608
gelu_cubic = 0.044715
bf16, f32 = jnp.bfloat16, jnp.float32
MESH = pl.DeviceIdType.MESH


def gelu_pair(pre_gelu):
    inner = gelu_scale * (pre_gelu + gelu_cubic * pre_gelu * pre_gelu * pre_gelu)
    tanh_part = jnp.tanh(inner)
    gelu_value = 0.5 * pre_gelu * (1.0 + tanh_part)
    gelu_slope = 0.5 * (1.0 + tanh_part) + 0.5 * pre_gelu * (
        1.0 - tanh_part * tanh_part
    ) * gelu_scale * (1.0 + 3.0 * gelu_cubic * pre_gelu * pre_gelu)
    return (gelu_value, gelu_slope)


def dot(a, b):
    return jnp.dot(a, b, preferred_element_type=f32)


def dot_nt(a, b):
    return lax.dot_general(a, b, (((1,), (1,)), ((), ())), preferred_element_type=f32)


def ticks_kernel(
    sections, tensors, replicas, own, ticks,
    inputs_hbm, pool_hbm, ids_hbm, seed_hbm, loss_hbm, proj_hbm, up_hbm, down_hbm,
    inputs_t, pool, act_t, sum_hidden, sum_grad, sum_up, out_t,
    proj, up, down, in_src, pool_src, ids_src, seed_src, loss_src, ids, loss_t,
    upstream, grads, hidden, part, got, own_part, slope_hi, slope_lo, slope, edge, edge_got,
    acc_hidden, acc_grad, acc_up,
    load_sem, place_sem, pool_sems, inputs_sems, ids_sems, loss_sems, seed_sems,
    part_sems, grad_sems, up_sems, edge_sems, out_sems,
):
    members = tensors * replicas
    section = lax.axis_index("section")
    tensor = lax.axis_index("tensor")
    replica = lax.axis_index("replica")
    me = tensor * replicas + replica
    hidden_rows = down.shape[0]

    def device(s, member):
        return {
            "section": s,
            "tensor": lax.div(member, replicas),
            "replica": lax.rem(member, replicas),
        }

    def member_at(by):
        return lax.rem(me + by, members)

    def replica_at(by):
        return lax.rem(replica + by, replicas)

    def load(i, src, dst):
        copy = pltpu.make_async_copy(src, dst, load_sem.at[i])
        copy.start()
        return copy

    pairs = [
        (pool_hbm, pool_src), (seed_hbm, seed_src), (ids_hbm, ids_src), (inputs_hbm, in_src),
        (loss_hbm, loss_src), (up_hbm, up), (down_hbm, down), (proj_hbm, proj),
    ]
    loads = [load(i, src, dst) for i, (src, dst) in enumerate(pairs)]
    ld_pool, ld_seed, ld_ids, ld_in, ld_loss, ld_up, ld_down, ld_proj = loads

    barrier = pltpu.get_barrier_semaphore()
    above = lax.rem(section + 1, sections)
    below = lax.rem(section + sections - 1, sections)
    mirror = sections - 1 - section
    for by in range(1, members):
        pl.semaphore_signal(barrier, 1, device_id=device(section, member_at(by)), device_id_type=MESH)
    for other in (above, below, mirror):
        pl.semaphore_signal(barrier, 1, device_id=device(other, me), device_id_type=MESH)
    pl.semaphore_wait(barrier, members - 1 + 3)

    sent = []

    def send(src, dst, sems, index, target):
        copy = pltpu.make_async_remote_copy(
            src_ref=src, dst_ref=dst, send_sem=sems.at[(0,) + index], recv_sem=sems.at[(1,) + index],
            device_id=target, device_id_type=MESH,
        )
        copy.start()
        sent.append(copy)
        return copy

    def over_replicas(src_of, dst, sems):
        return [
            send(src_of(replica_at(by)), dst, sems, (by - 1,),
                 device(section, tensor * replicas + replica_at(by)))
            for by in range(1, replicas)
        ]

    def place(i, src, dst):
        copy = pltpu.make_async_copy(src, dst, place_sem.at[i])
        copy.start()
        return copy

    slab = pl.ds(pl.multiple_of(me * own, 16), own)
    wide = pl.ds(pl.multiple_of(tensor * (replicas * own), 16), replicas * own)
    ld_pool.wait()
    pool_in = over_replicas(lambda r: pool_src, pool.at[replica], pool_sems)
    places = [place(0, pool_src, pool.at[replica])]
    ld_seed.wait()
    seed_to = upstream.at[0, replica, wide]
    seed_in = [
        send(seed_src, seed_to, seed_sems, (by - 1,), device(section, member_at(by)))
        for by in range(1, members)
    ]
    places.append(place(1, seed_src, seed_to))
    ld_ids.wait()
    ids_in = over_replicas(lambda r: ids_src, ids.at[replica], ids_sems)
    places.append(place(2, ids_src, ids.at[replica]))
    ld_in.wait()
    inputs_in = over_replicas(lambda r: in_src.at[r], inputs_t.at[replica], inputs_sems)
    places.append(place(3, in_src.at[replica], inputs_t.at[replica]))
    ld_loss.wait()
    loss_in = over_replicas(lambda r: loss_src.at[r], loss_t.at[replica], loss_sems)
    places.append(place(4, loss_src.at[replica], loss_t.at[replica]))

    acc_hidden[...] = jnp.zeros_like(acc_hidden)
    acc_grad[...] = jnp.zeros_like(acc_grad)
    acc_up[...] = jnp.zeros_like(acc_up)

    ld_up.wait()
    places[0].wait()
    for copy in pool_in:
        copy.wait_recv()
    step = 128

    for r in range(replicas):
        def pre_step(c, carry, r=r):
            cols = pl.ds(pl.multiple_of(c * step, step), step)
            value, gelu_slope = gelu_pair(dot(pool[r], up[:, cols]).T)
            act_t[r, cols, :] = value.astype(bf16)
            high = gelu_slope.astype(bf16)
            slope_hi[r, cols, :] = high
            slope_lo[r, cols, :] = (gelu_slope - high.astype(f32)).astype(bf16)
            return carry
        lax.fori_loop(0, hidden_rows // step, pre_step, 0)

    places[2].wait()
    for copy in ids_in:
        copy.wait_recv()

    def picks(t, r):
        row = ids[r, pl.ds(t, 1), :]
        place_of = lax.broadcasted_iota(jnp.int32, (pool.shape[1], row.shape[1]), 0)
        return jnp.where(place_of == row, 1.0, 0.0).astype(bf16)

    def pick_slope(t, r):
        chosen = picks(t, r)
        slope[r] = dot(slope_hi[r], chosen) + dot(slope_lo[r], chosen)

    for r in range(replicas):
        pick_slope(0, r)

    ld_down.wait()
    ld_proj.wait()
    places[1].wait()
    for copy in seed_in:
        copy.wait_recv()

    up_in = {}
    part_in, grad_in, edge_in = {}, {}, {}

    def stage_hidden(t, r):
        for copy in up_in.get((t, r), ()):
            copy.wait_recv()
        hidden[t, r] = (dot(down[...], upstream[t, r]) * slope[r]).astype(bf16)
        copies = []
        for by in range(1, members):
            to = member_at(by)
            rows = pl.ds(pl.multiple_of(to * own, 16), own)
            part[t, r, by - 1] = dot(up[rows, :], hidden[t, r]).astype(bf16)
            copies.append(send(part.at[t, r, by - 1], got.at[t, r, by - 1], part_sems,
                               (t, r, by - 1), device(section, to)))
        own_part[r] = dot(up[slab, :], hidden[t, r]) + upstream[t, r, slab, :].astype(f32)
        part_in[t, r] = copies

    def stage_sum(t, r):
        total = own_part[r]
        for by in range(1, members):
            part_in[t, r][by - 1].wait_recv()
            total = total + got[t, r, by - 1].astype(f32)
        grads[t, r, slab, :] = total.astype(bf16)
        mine = grads.at[t, r, slab]
        grad_in[t, r] = [
            send(mine, mine, grad_sems, (t, r, by - 1), device(section, member_at(by)))
            for by in range(1, members)
        ]

    def stage_project(t, r):
        for copy in grad_in[t, r]:
            copy.wait_recv()
        edge[t, r, 1] = dot(proj[1], grads[t, r]).astype(bf16)
        last = t + 1 == ticks
        if not last:
            skip = pltpu.make_async_remote_copy(
                src_ref=edge.at[t, r, 1], dst_ref=edge_got.at[t, r, 1],
                send_sem=edge_sems.at[0, t, r, 1], recv_sem=edge_sems.at[1, t, r, 1],
                device_id=device(mirror, me), device_id_type=MESH,
            )
            pl.when(section >= sections // 2)(skip.start)
        edge[t, r, 0] = dot(proj[0], grads[t, r]).astype(bf16)
        if not last:
            down_copy = pltpu.make_async_remote_copy(
                src_ref=edge.at[t, r, 0], dst_ref=edge_got.at[t, r, 0],
                send_sem=edge_sems.at[0, t, r, 0], recv_sem=edge_sems.at[1, t, r, 0],
                device_id=device(below, me), device_id_type=MESH,
            )
            pl.when(section > 0)(down_copy.start)
            edge_in[t, r] = (down_copy, skip)

    def stage_next(t, r):
        down_copy, skip = edge_in[t, r]

        @pl.when(section < sections // 2)
        def _():
            down_copy.wait_recv()
            skip.wait_recv()
            summed = edge_got[t, r, 0].astype(f32) + edge_got[t, r, 1].astype(f32)
            upstream[t + 1, r, slab, :] = summed.astype(bf16)

        @pl.when((section >= sections // 2) & (section < sections - 1))
        def _():
            down_copy.wait_recv()
            upstream[t + 1, r, slab, :] = edge_got[t, r, 0]

        @pl.when(section == sections - 1)
        def _():
            upstream[t + 1, r, slab, :] = loss_t[r, t]

        mine = upstream.at[t + 1, r, slab]
        up_in[t + 1, r] = [
            send(mine, mine, up_sems, (t, r, by - 1), device(section, member_at(by)))
            for by in range(1, members)
        ]

    every = range(replicas)
    for t in range(ticks):
        for r in every:
            stage_hidden(t, r)
        for r in every:
            stage_sum(t, r)
        for r in every:
            chosen = picks(t, r)
            acc_hidden[r] += dot_nt(chosen, hidden[t, r])
            acc_up[r] += dot_nt(chosen, upstream[t, r])
        if t + 1 < ticks:
            for r in every:
                pick_slope(t + 1, r)
        if t == 0:
            places[3].wait()
            places[4].wait()
            for copy in inputs_in + loss_in:
                copy.wait_recv()
        for r in every:
            stage_project(t, r)
        for r in every:
            if t + 1 < ticks:
                stage_next(t, r)
        for r in every:
            acc_grad[r] += dot_nt(picks(t, r), grads[t, r])

    last = ticks - 1
    outs = []
    for by in range(1, replicas):
        to = replica_at(by)
        outs.append(send(edge.at[last, to], out_t.at[replica], out_sems, (by - 1,),
                         device(section, tensor * replicas + to)))
    out_place = place(5, edge.at[last, replica], out_t.at[replica])
    sum_hidden[...] = acc_hidden[...].astype(bf16)
    sum_grad[...] = acc_grad[...].astype(bf16)
    sum_up[...] = acc_up[...].astype(bf16)
    for copy in outs:
        copy.wait_recv()
    out_place.wait()
    for copy in sent:
        copy.wait_send()
    for key in edge_in:
        down_copy, skip = edge_in[key]
        pl.when(section > 0)(down_copy.wait_send)
        pl.when(section >= sections // 2)(skip.wait_send)


def body(pool_inputs, pool_mixed, crop_ids, incoming, loss_grads, w_proj, w_up, w_down):
    sections = lax.axis_size("section")
    tensors, replicas = lax.axis_size("tensor"), lax.axis_size("replica")
    members = tensors * replicas
    encoder = lax.axis_index("section") < sections // 2
    own = w_proj.shape[2]
    own_p = -(-own // 16) * 16
    rows, width = incoming.shape[1], w_up.shape[1]
    width_p = members * own_p
    hidden = w_up.shape[2]
    ticks = crop_ids.shape[1]
    saved = pool_mixed.shape[1]

    def padded(x, axis):
        if own == own_p:
            return x
        count = x.shape[axis] // own
        shape = x.shape[:axis] + (count, own) + x.shape[axis + 1:]
        fill = [(0, 0)] * (x.ndim + 1)
        fill[axis + 1] = (0, own_p - own)
        shape_p = x.shape[:axis] + (count * own_p,) + x.shape[axis + 1:]
        return jnp.pad(x.reshape(shape), fill).reshape(shape_p)

    proj = padded(padded(w_proj[0], 1), 2)
    up, down = padded(w_up[0], 0), padded(w_down[0], 1)
    pool_own = padded(pool_mixed[0], 1)
    mask = jnp.stack([jnp.ones((), bf16), jnp.where(encoder, 0.0, 1.0).astype(bf16)])
    features = (pool_inputs[0] * mask[None, :, None]).transpose(1, 2, 0)
    features = features.reshape(2, replicas, own, saved).transpose(1, 0, 2, 3)
    features = padded(features, 2)
    seed = padded(incoming[0].T, 0)
    loss = loss_grads.transpose(0, 2, 1).reshape(ticks - 1, replicas, own, rows)
    loss = padded(loss.transpose(1, 0, 2, 3), 2)

    shape = jax.ShapeDtypeStruct
    vmem = pl.BlockSpec(memory_space=pltpu.VMEM)
    hbm = pl.BlockSpec(memory_space=pl.ANY)
    dma = pltpu.SemaphoreType.DMA
    scratch = [
        pltpu.VMEM(proj.shape, bf16), pltpu.VMEM(up.shape, bf16), pltpu.VMEM(down.shape, bf16),
        pltpu.VMEM(features.shape, bf16), pltpu.VMEM(pool_own.shape, bf16),
        pltpu.VMEM(crop_ids.shape[1:], jnp.int32), pltpu.VMEM(seed.shape, bf16),
        pltpu.VMEM(loss.shape, bf16), pltpu.VMEM((replicas,) + crop_ids.shape[1:], jnp.int32),
        pltpu.VMEM((replicas, ticks - 1, own_p, rows), bf16),
        pltpu.VMEM((ticks, replicas, width_p, rows), bf16),
        pltpu.VMEM((ticks, replicas, width_p, rows), bf16),
        pltpu.VMEM((ticks, replicas, hidden, rows), bf16),
        pltpu.VMEM((ticks, replicas, members - 1, own_p, rows), bf16),
        pltpu.VMEM((ticks, replicas, members - 1, own_p, rows), bf16),
        pltpu.VMEM((replicas, own_p, rows), f32),
        pltpu.VMEM((replicas, hidden, saved), bf16), pltpu.VMEM((replicas, hidden, saved), bf16),
        pltpu.VMEM((replicas, hidden, rows), f32),
        pltpu.VMEM((ticks, replicas, 2, own_p, rows), bf16),
        pltpu.VMEM((ticks - 1, replicas, 2, own_p, rows), bf16),
        pltpu.VMEM((replicas, saved, hidden), f32), pltpu.VMEM((replicas, saved, width_p), f32),
        pltpu.VMEM((replicas, saved, width_p), f32),
        dma((8,)), dma((6,)), dma((2, replicas - 1)), dma((2, replicas - 1)), dma((2, replicas - 1)),
        dma((2, replicas - 1)), dma((2, members - 1)),
        dma((2, ticks, replicas, members - 1)), dma((2, ticks, replicas, members - 1)),
        dma((2, ticks - 1, replicas, members - 1)), dma((2, ticks - 1, replicas, 2)),
        dma((2, replicas - 1)),
    ]
    inputs_t, pool, act_t, sum_hidden, sum_grad, sum_up, out_t = pl.pallas_call(
        functools.partial(ticks_kernel, sections, tensors, replicas, own_p, ticks),
        out_shape=(
            shape((replicas, 2, own_p, saved), bf16),
            shape((replicas, saved, width_p), bf16),
            shape((replicas, hidden, saved), bf16),
            shape((replicas, saved, hidden), bf16),
            shape((replicas, saved, width_p), bf16),
            shape((replicas, saved, width_p), bf16),
            shape((replicas, 2, own_p, rows), bf16),
        ),
        in_specs=[hbm] * 8,
        out_specs=(vmem,) * 7,
        scratch_shapes=scratch,
        compiler_params=pltpu.CompilerParams(
            collective_id=0, has_side_effects=True, vmem_limit_bytes=60 * 1024 * 1024
        ),
        name="ticks",
    )(features, pool_own, crop_ids[0], seed, loss, proj, up, down)

    def trimmed(x, axis):
        if own == own_p:
            return x
        count = x.shape[axis] // own_p
        x = x.reshape(x.shape[:axis] + (count, own_p) + x.shape[axis + 1:])
        x = lax.slice_in_dim(x, 0, own, axis=axis + 1)
        return x.reshape(x.shape[:axis] + (count * own,) + x.shape[axis + 2:])

    def finish(spec, left, right):
        total = 0.0
        for r in range(replicas):
            one = jnp.einsum(spec, left[r], right[r], preferred_element_type=f32)
            total = total + one.astype(bf16).astype(f32)
        return total.astype(bf16)

    grad_down = trimmed(finish("fp,pd->fd", act_t, sum_up), 1)[None]
    grad_up = trimmed(finish("pd,pf->df", pool, sum_hidden), 0)[None]
    grad_proj = trimmed(trimmed(finish("kip,pj->kij", inputs_t, sum_grad), 1), 2)[None]
    outgoing = trimmed(out_t, 2).transpose(3, 1, 0, 2).reshape(rows, 2, replicas * own)
    return grad_proj, grad_up, grad_down, outgoing[None]


def solution(mesh):
    in_specs = (
        P("section", "replica", None, "tensor"),
        P("section", "replica", None),
        P("section", "replica", None),
        P("section", "replica", "tensor"),
        P(None, "replica", "tensor"),
        P("section", None, ("tensor", "replica"), None),
        P("section", None, ("tensor", "replica")),
        P("section", ("tensor", "replica"), None),
    )
    out_specs = (
        P("section", None, ("tensor", "replica"), None),
        P("section", None, ("tensor", "replica")),
        P("section", ("tensor", "replica"), None),
        P("section", "replica", None, "tensor"),
    )
    return jax.shard_map(body, mesh=mesh, in_specs=in_specs, out_specs=out_specs, check_vma=False)
```

profile of v0, /device:TPU:0, one launch (start us, length us, event | category | flops | bytes accessed | tf_op | source)
XLA Modules:
  0.0 155.3 jit_solution(3914589545052280836)
XLA Ops:
  0.6 0.1 pad_maximum_fusion
  0.7 1.1 bitcast_multiply_fusion
  1.8 0.8 copy.18
  2.6 1.9 %copy.17 = bf16[3,2,352,128]{3,2,0,1:T(8,128)(2,1)} copy(bf16[3,2,352,128]{3,2,1,0:T(8,128)(2,1)} %bitcast.75) | data formatting | bytes 1081344 | tf_op jit(solution)/shard_map/reshape | solution.py:328
  4.4 140.6 %ticks.1 = (bf16[2,2,352,128]{3,2,1,0:T(8,128)(2,1)}, bf16[2,128,1408]{2,1,0:T(8,128)(2,1)}, bf16[2,768,128]{2,1,0:T(8,128)(2,1)}, bf16[2,128,768]{2,1,0:T(8,128...) custom-call(bf16[2,2,352,128]{3,2,1,0:T(8,128)(2,1)} %bitcast.73, ...), custom_call_target="tpu_custom_call" | custom-call | tf_op jit(solution)/shard_map/ticks/pallas_call | solution.py:359
  145.1 0.0 copy-start.2
  145.1 0.0 copy-start.4
  145.1 1.9 %convolution_convert_fusion = bf16[768,1408]{1,0:T(8,128)(2,1)S(1)} fusion(bf16[2,128,1408]{2,1,0:T(8,128)(2,1)} %get-tuple-element.16, bf16[2,768,128]{2,1,0:T(8,128)(2,1)} %get-tuple-element.15), kind=kOutput, calls=%fused_computation.3 | convolution fusion | flops 277905408 | bytes 2719744 | tf_op jit(solution)/shard_map/fp,pd->fd/dot_general | solution.py:390
  147.0 0.0 copy-done.2
  147.0 0.0 copy-done.4
  147.0 0.0 copy-start.1
  147.0 0.0 copy-start.3
  147.0 2.1 %fusion.1 = bf16[1,768,1408]{2,1,0:T(8,128)(2,1)} fusion(bf16[768,1408]{1,0:T(8,128)(2,1)S(1)} %convolution_convert_fusion, bf16[2,128,1408]{2,1,0:T(8,128)(2,1)S(1)} %copy-done.2, bf16[2,768,128]{2,1,0:T(8,128)(2,1)S(1)} %copy-done.4), kind=kOutput, calls=%fused_computation.10 | convolution fusion | flops 282230784 | bytes 4882432 | tf_op jit(solution)/shard_map/fp,pd->fd/dot_general | solution.py:390
  149.1 0.0 copy-done.1
  149.1 0.0 copy-done.3
  149.1 0.8 convolution_convert_fusion.2
  149.8 0.0 copy-start
  149.8 0.0 copy-start.5
  149.8 2.1 %fusion = bf16[1,1408,768]{2,1,0:T(8,128)(2,1)} fusion(bf16[1408,768]{1,0:T(8,128)(2,1)S(1)} %convolution_convert_fusion.2, bf16[2,128,1408]{2,1,0:T(8,128)(2,1)S(1)} %copy-done.1, bf16[2,128,768]{2,1,0:T(8,128)(2,1)S(1)} %copy-done.3), kind=kOutput, calls=%fused_computation.9 | convolution fusion | flops 282230784 | bytes 4882432 | tf_op jit(solution)/shard_map/pd,pf->df/dot_general | solution.py:390
  151.9 0.0 copy-done
  151.9 0.0 copy-done.5
  151.9 0.7 convolution_convert_fusion.4
  152.6 0.0 copy-start.6
  152.6 1.9 %fusion.2 = bf16[1,2,352,1408]{3,2,1,0:T(8,128)(2,1)} fusion(bf16[2,352,1408]{2,1,0:T(8,128)(2,1)S(1)} %convolution_convert_fusion.4, bf16[2,128,1408]{2,1,0:T(8,128)(2,1)S(1)} %copy-done, bf16[2,2,352,128]{3,2,1,0:T(8,128)(2,1)S(1)} %copy-done.5), kind=kOutput, calls=%fused_computation.11 | convolution fusion | flops 258711552 | bytes 4505600 | tf_op jit(solution)/shard_map/kip,pj->kij/dot_general | solution.py:390
  154.6 0.0 copy-done.6
  154.6 0.8 copy.14
Async XLA Ops:
  145.1 1.9 %copy-start.2 = (bf16[2,128,1408]{2,1,0:T(8,128)(2,1)S(1)}, bf16[2,128,1408]{2,1,0:T(8,128)(2,1)}, u32[]{:S(2)}) copy-start(bf16[2,128,1408]{2,1,0:T(8,128)(2,1)} %get-tuple-element.16) | copy-start | bytes 2162692
  145.1 1.9 %copy-start.4 = (bf16[2,768,128]{2,1,0:T(8,128)(2,1)S(1)}, bf16[2,768,128]{2,1,0:T(8,128)(2,1)}, u32[]{:S(2)}) copy-start(bf16[2,768,128]{2,1,0:T(8,128)(2,1)} %get-tuple-element.15) | copy-start | bytes 1179652
  147.0 2.1 %copy-start.1 = (bf16[2,128,1408]{2,1,0:T(8,128)(2,1)S(1)}, bf16[2,128,1408]{2,1,0:T(8,128)(2,1)}, u32[]{:S(2)}) copy-start(bf16[2,128,1408]{2,1,0:T(8,128)(2,1)} %get-tuple-element.13) | copy-start | bytes 2162692
  147.0 2.1 %copy-start.3 = (bf16[2,128,768]{2,1,0:T(8,128)(2,1)S(1)}, bf16[2,128,768]{2,1,0:T(8,128)(2,1)}, u32[]{:S(2)}) copy-start(bf16[2,128,768]{2,1,0:T(8,128)(2,1)} %get-tuple-element.14) | copy-start | bytes 1179652
  149.8 2.1 %copy-start = (bf16[2,128,1408]{2,1,0:T(8,128)(2,1)S(1)}, bf16[2,128,1408]{2,1,0:T(8,128)(2,1)}, u32[]{:S(2)}) copy-start(bf16[2,128,1408]{2,1,0:T(8,128)(2,1)} %get-tuple-element.12) | copy-start | bytes 2162692
  149.8 2.1 %copy-start.5 = (bf16[2,2,352,128]{3,2,1,0:T(8,128)(2,1)S(1)}, bf16[2,2,352,128]{3,2,1,0:T(8,128)(2,1)}, u32[]{:S(2)}) copy-start(bf16[2,2,352,128]{3,2,1,0:T(8,128)(2,1)} %get-tuple-element.11) | copy-start | bytes 1081348
  152.6 2.0 %copy-start.6 = (bf16[2,2,352,128]{3,2,1,0:T(8,128)(2,1)S(1)}, bf16[2,2,352,128]{3,2,1,0:T(8,128)(2,1)}, u32[]{:S(2)}) copy-start(bf16[2,2,352,128]{3,2,1,0:T(8,128)(2,1)} %get-tuple-element.17) | copy-start | bytes 1081348
where the time goes:
time: 156 us; the launch traced here: 155 us
  Pallas kernels  141 us (90%)
  matrix products  9.39 us (6%)
  local copies, waits for them, and re-layouts  3.43 us (2%)
    pallas_call x1, Pallas kernels, body(): pl.pallas_call(functools.partial(ticks_kernel, sections, tensors, replica...  141 us
    dot_general x6, matrix products, finish(): one = jnp.einsum(spec, left[r], right[r], preferred_element_type=f32)  9.39 us

commit v1 on v0

--- a/solution.py
+++ b/solution.py
@@ -111,6 +111,8 @@
     ld_pool.wait()
     pool_in = over_replicas(lambda r: pool_src, pool.at[replica], pool_sems)
     places = [place(0, pool_src, pool.at[replica])]
+    ld_ids.wait()
+    ids_in = over_replicas(lambda r: ids_src, ids.at[replica], ids_sems)
     ld_seed.wait()
     seed_to = upstream.at[0, replica, wide]
     seed_in = [
@@ -118,15 +120,20 @@
         for by in range(1, members)
     ]
     places.append(place(1, seed_src, seed_to))
-    ld_ids.wait()
-    ids_in = over_replicas(lambda r: ids_src, ids.at[replica], ids_sems)
     places.append(place(2, ids_src, ids.at[replica]))
     ld_in.wait()
-    inputs_in = over_replicas(lambda r: in_src.at[r], inputs_t.at[replica], inputs_sems)
     places.append(place(3, in_src.at[replica], inputs_t.at[replica]))
     ld_loss.wait()
-    loss_in = over_replicas(lambda r: loss_src.at[r], loss_t.at[replica], loss_sems)
     places.append(place(4, loss_src.at[replica], loss_t.at[replica]))
+    is_top = section == sections - 1
+    loss_in = []
+    for by in range(1, replicas):
+        to = replica_at(by)
+        loss_in.append(pltpu.make_async_remote_copy(
+            src_ref=loss_src.at[to], dst_ref=loss_t.at[replica],
+            send_sem=loss_sems.at[0, by - 1], recv_sem=loss_sems.at[1, by - 1],
+            device_id=device(section, tensor * replicas + to), device_id_type=MESH,
+        ))
 
     acc_hidden[...] = jnp.zeros_like(acc_hidden)
     acc_grad[...] = jnp.zeros_like(acc_grad)
@@ -134,20 +141,26 @@
 
     ld_up.wait()
     places[0].wait()
-    for copy in pool_in:
-        copy.wait_recv()
     step = 128
 
-    for r in range(replicas):
-        def pre_step(c, carry, r=r):
-            cols = pl.ds(pl.multiple_of(c * step, step), step)
+    for by in range(replicas):
+        r = lax.rem(replica + replicas - by, replicas)
+        if by > 0:
+            pool_in[by - 1].wait_recv()
+
+        def pre_at(cols, r=r):
             value, gelu_slope = gelu_pair(dot(pool[r], up[:, cols]).T)
             act_t[r, cols, :] = value.astype(bf16)
             high = gelu_slope.astype(bf16)
             slope_hi[r, cols, :] = high
             slope_lo[r, cols, :] = (gelu_slope - high.astype(f32)).astype(bf16)
-            return carry
-        lax.fori_loop(0, hidden_rows // step, pre_step, 0)
+
+        @pl.loop(0, hidden_rows // step)
+        def _(c):
+            pre_at(pl.ds(pl.multiple_of(c * step, step), step))
+
+        if hidden_rows % step:
+            pre_at(pl.ds(hidden_rows - hidden_rows % step, hidden_rows % step))
 
     places[2].wait()
     for copy in ids_in:
@@ -251,6 +264,9 @@
     for t in range(ticks):
         for r in every:
             stage_hidden(t, r)
+        if t == 0:
+            for copy in loss_in:
+                pl.when(is_top)(copy.start)
         for r in every:
             stage_sum(t, r)
         for r in every:
@@ -261,12 +277,13 @@
             for r in every:
                 pick_slope(t + 1, r)
         if t == 0:
-            places[3].wait()
             places[4].wait()
-            for copy in inputs_in + loss_in:
-                copy.wait_recv()
+            for copy in loss_in:
+                pl.when(is_top)(copy.wait_recv)
         for r in every:
             stage_project(t, r)
+        if t == min(1, ticks - 1):
+            inputs_in = over_replicas(lambda r: in_src.at[r], inputs_t.at[replica], inputs_sems)
         for r in every:
             if t + 1 < ticks:
                 stage_next(t, r)
@@ -283,15 +300,51 @@
     sum_hidden[...] = acc_hidden[...].astype(bf16)
     sum_grad[...] = acc_grad[...].astype(bf16)
     sum_up[...] = acc_up[...].astype(bf16)
-    for copy in outs:
+    for copy in outs + inputs_in:
         copy.wait_recv()
     out_place.wait()
+    places[3].wait()
+    for copy in loss_in:
+        pl.when(is_top)(copy.wait_send)
     for copy in sent:
         copy.wait_send()
     for key in edge_in:
         down_copy, skip = edge_in[key]
         pl.when(section > 0)(down_copy.wait_send)
         pl.when(section >= sections // 2)(skip.wait_send)
+
+
+def tail_kernel(
+    replicas, keep_ref, act_t, pool, inputs_t, sum_hidden, sum_grad, sum_up,
+    down_out, up_out, proj_out, down_v, up_v, proj_v, sems,
+):
+    copies = []
+
+    def finish(term, rows, kept, out, scale=None):
+        total = 0.0
+        for r in range(replicas):
+            total = total + term(r).astype(bf16).astype(f32)
+        if scale is not None:
+            total = total * scale
+        kept.at[rows][...] = total.astype(bf16)
+        copy = pltpu.make_async_copy(kept.at[rows], out.at[rows], sems.at[len(copies)])
+        copy.start()
+        copies.append(copy)
+
+    for start in range(0, down_v.shape[0], 128):
+        rows = pl.ds(start, min(128, down_v.shape[0] - start))
+        finish(lambda r: dot(act_t[r, rows, :], sum_up[r]), rows, down_v, down_out)
+    half = proj_v.shape[1] // 2
+    for k in range(2):
+        for start in (0, half):
+            rows = (k, pl.ds(start, half))
+            finish(lambda r: dot(inputs_t[r, k, pl.ds(start, half), :], sum_grad[r]), rows,
+                   proj_v, proj_out, keep_ref[0] if k else None)
+    for start in range(0, up_v.shape[0], 128):
+        rows = pl.ds(start, min(128, up_v.shape[0] - start))
+        finish(lambda r: dot(pool[r, :, rows].T, sum_hidden[r]), rows, up_v, up_out)
+    for copy in copies:
+        copy.wait()
 
 
 def body(pool_inputs, pool_mixed, crop_ids, incoming, loss_grads, w_proj, w_up, w_down):
@@ -320,8 +373,8 @@
     proj = padded(padded(w_proj[0], 1), 2)
     up, down = padded(w_up[0], 0), padded(w_down[0], 1)
     pool_own = padded(pool_mixed[0], 1)
-    mask = jnp.stack([jnp.ones((), bf16), jnp.where(encoder, 0.0, 1.0).astype(bf16)])
-    features = (pool_inputs[0] * mask[None, :, None]).transpose(1, 2, 0)
+    keep = jnp.where(encoder, 0.0, 1.0).astype(f32)[None]
+    features = pool_inputs[0].transpose(1, 2, 0)
     features = features.reshape(2, replicas, own, saved).transpose(1, 0, 2, 3)
     features = padded(features, 2)
     seed = padded(incoming[0].T, 0)
@@ -384,16 +437,25 @@
         x = lax.slice_in_dim(x, 0, own, axis=axis + 1)
         return x.reshape(x.shape[:axis] + (count * own,) + x.shape[axis + 2:])
 
-    def finish(spec, left, right):
-        total = 0.0
-        for r in range(replicas):
-            one = jnp.einsum(spec, left[r], right[r], preferred_element_type=f32)
-            total = total + one.astype(bf16).astype(f32)
-        return total.astype(bf16)
-
-    grad_down = trimmed(finish("fp,pd->fd", act_t, sum_up), 1)[None]
-    grad_up = trimmed(finish("pd,pf->df", pool, sum_hidden), 0)[None]
-    grad_proj = trimmed(trimmed(finish("kip,pj->kij", inputs_t, sum_grad), 1), 2)[None]
+    grad_down, grad_up, grad_proj = pl.pallas_call(
+        functools.partial(tail_kernel, replicas),
+        out_shape=(
+            shape((hidden, width_p), bf16), shape((width_p, hidden), bf16),
+            shape((2, own_p, width_p), bf16),
+        ),
+        in_specs=[pl.BlockSpec(memory_space=pltpu.SMEM)] + [vmem] * 6,
+        out_specs=(hbm,) * 3,
+        scratch_shapes=[
+            pltpu.VMEM((hidden, width_p), bf16), pltpu.VMEM((width_p, hidden), bf16),
+            pltpu.VMEM((2, own_p, width_p), bf16),
+            dma((-(-hidden // 128) - (-width_p // 128) + 4,)),
+        ],
+        compiler_params=pltpu.CompilerParams(vmem_limit_bytes=40 * 1024 * 1024),
+        name="tail",
+    )(keep, act_t, pool, inputs_t, sum_hidden, sum_grad, sum_up)
+    grad_down = trimmed(grad_down, 1)[None]
+    grad_up = trimmed(grad_up, 0)[None]
+    grad_proj = trimmed(trimmed(grad_proj, 1), 2)[None]
     outgoing = trimmed(out_t, 2).transpose(3, 1, 0, 2).reshape(rows, 2, replicas * own)
     return grad_proj, grad_up, grad_down, outgoing[None]
 

time: 156 us -> 159 us (1.019); the launches traced: 155 us -> 156 us
  matrix products: 9.39 us -> 0 us
  local copies, waits for them, and re-layouts: 3.43 us -> 11.7 us
  Pallas kernels: 141 us -> 143 us
    dot_general x6 -> x0, matrix products: 9.39 us -> none  [finish(): one = jnp.einsum(spec, left[r], right[r], preferred_element_type=f32)]
    unnamed x14 -> x12, local copies, waits for them, and re-layouts: 0.03 us -> 6.3 us
    pallas_call x0 -> x1, Pallas kernels: none -> 4.45 us  [body(): pl.pallas_call(functools.partial(tail_kernel, replicas), out_shape=(shape...]
    pallas_call x1, Pallas kernels: 141 us -> 139 us  [body(): pl.pallas_call(functools.partial(ticks_kernel, sections, tensors, replica...]
where the time goes in v1:
time: 159 us; the launch traced here: 156 us
  Pallas kernels  143 us (90%)
  local copies, waits for them, and re-layouts  11.7 us (7%)
    pallas_call x1, Pallas kernels, body(): pl.pallas_call(functools.partial(ticks_kernel, sections, tensors, replica...  139 us
    unnamed x12, local copies, waits for them, and re-layouts  6.3 us
    pallas_call x1, Pallas kernels, body(): pl.pallas_call(functools.partial(tail_kernel, replicas), out_shape=(shape...  4.45 us

profile of v1, /device:TPU:0, one launch (start us, length us, event | category | flops | bytes accessed | tf_op | source)
XLA Modules:
  0.0 155.8 jit_solution(5619811185704881147)
XLA Ops:
  0.6 1.7 %copy.18 = bf16[2,2,352,128]{3,2,0,1:T(8,128)(2,1)} copy(bf16[2,2,352,128]{3,2,1,0:T(8,128)(2,1)} %bitcast.35) | data formatting | bytes 720896 | tf_op jit(solution)/shard_map/reshape | solution.py:378
  2.4 1.9 %copy.17 = bf16[3,2,352,128]{3,2,0,1:T(8,128)(2,1)} copy(bf16[3,2,352,128]{3,2,1,0:T(8,128)(2,1)} %bitcast.33) | data formatting | bytes 1081344 | tf_op jit(solution)/shard_map/reshape | solution.py:381
  4.3 138.8 %ticks.1 = (bf16[2,2,352,128]{3,2,1,0:T(8,128)(2,1)}, bf16[2,128,1408]{2,1,0:T(8,128)(2,1)}, bf16[2,768,128]{2,1,0:T(8,128)(2,1)}, bf16[2,128,768]{2,1,0:T(8,128...) custom-call(bf16[2,2,352,128]{3,2,1,0:T(8,128)(2,1)} %bitcast.32, ...), custom_call_target="tpu_custom_call" | custom-call | tf_op jit(solution)/shard_map/ticks/pallas_call | solution.py:412
  143.1 1.7 %copy.14 = bf16[128,2,2,352]{0,3,2,1:T(8,128)(2,1)} copy(bf16[128,2,2,352]{0,3,1,2:T(8,128)(2,1)} %bitcast.37) | data formatting | bytes 720896 | tf_op jit(solution)/shard_map/transpose | solution.py:459
  144.9 0.0 copy-start
  144.9 1.1 copy-done
  146.0 0.0 copy-start.1
  146.0 1.1 copy-done.1
  147.1 0.0 copy-start.2
  147.1 1.1 copy-done.2
  148.2 0.0 copy-start.3
  148.2 1.0 copy-done.3
  149.2 0.0 copy-start.4
  149.2 1.0 copy-done.4
  150.2 0.0 copy-start.5
  150.2 1.0 copy-done.5
  151.2 4.5 %tail.1 = (bf16[768,1408]{1,0:T(8,128)(2,1)}, bf16[1408,768]{1,0:T(8,128)(2,1)}, bf16[2,352,1408]{2,1,0:T(8,128)(2,1)}) custom-call(f32[1]{0:T(128)} %bitcast.keep_ref, bf16[2,768,128]{2,1,0:T(8,128)(2,1)S(1)} %copy-done.3, bf16[2,128,1408]{2,1,0:T(8,128)(2,1)S(1)} %copy-done, bf16[2,2,352,128]{3,2,1,0:T(8,128)(2,1)S(1)} %copy-done.5, ...), custom_call_target="tpu_custom_call" | custom-call | tf_op jit(solution)/shard_map/tail/pallas_call | solution.py:440
Async XLA Ops:
  144.9 1.1 copy-start
  146.0 1.1 copy-start.1
  147.1 1.1 copy-start.2
  148.2 1.0 copy-start.3
  149.2 1.0 copy-start.4
  150.2 1.0 copy-start.5
